TPU v7x, 32 devices: a whole 2x2x4 slice. The times are simulated.
32 devices in a mesh: cube: 4 (over z), row: 2 (over y), col: 4 (over x, core).
Axes of the slice: x: 2, y: 2, z: 4, core: 2. Of those that a mesh axis runs over, the one named last changes fastest.
Arguments:
- diag_block: float32 [4, 512, 512], P('cube', ('row', 'col')), may hold values from -1 to 4, as said below
- panel: float32 [4, 16384, 512], P('cube', 'row', 'col'), may hold values from -2 to 2
- pattern: int32 [4, 128, 4], P('cube', 'row', 'col'), may hold values 0 or 1
- contribution: float32 [4, 16384, 512], P('cube', 'row', 'col'), may hold values from -6 to 6
- route: int32 [4, 128, 1], P('cube', 'row'), may hold values from 0 to 3; in each aligned block of 64 rows (0 to 63, 64 to 127, ..., all dimensions but the last counted through in order) at most 32 rows name the same one
- slot: int32 [4, 128], P('cube', 'row'), may hold values from 0 to 31
Outputs:
- diag_factor: float32 [4, 512, 512], P('cube', ('row', 'col'))
- panel_factor: float32 [4, 16384, 512], P('cube', 'row', 'col')
- assembled: float32 [4, 8192, 512], P('cube', 'row', 'col')
Inputs may be any that keep to these rules, and one draw needn't show every extreme that they name: `diag_block`: each 512 x 512 block is symmetric with positive diagonal larger than the sum of magnitudes of the rest of its row. `route`: within the 64 rows of one device, no value names more than 32 blocks.
All inputs are finite; a program needn't handle non-finite values. No bound on the sum of `pattern` on one device may be relied on, other than what follows from the above.
Results may differ from a plain program's by a relative error of at most 0.0001.
Values sent between devices are 32-bit elements; how exact they have to be, the bound alone decides.
A program may use at most 128 MiB of HBM per device.

v0:
```python
import jax
import jax.numpy as jnp
from jax import lax
from jax.sharding import PartitionSpec as P

BS = 128


def from_root(value, axis, root):
    mine = lax.axis_index(axis) == root
    return lax.psum(jnp.where(mine, value, jnp.zeros_like(value)), axis)


def partner(value, axis, apart):
    mask = 2**apart
    pairs = [(source, source ^ mask) for source in range(lax.axis_size(axis))]
    return lax.ppermute(value, axis, pairs)


def on_device(diag_block, panel, pattern, contribution, route, slot):
    highest = lax.Precision.HIGHEST
    contract = (((1,), (1,)), ((), ()))
    whole = lax.all_gather(diag_block, ("row", "col"), axis=1, tiled=True)[0]
    width = whole.shape[0]
    lower = jnp.linalg.cholesky(whole)
    inverse = jax.scipy.linalg.solve_triangular(
        lower, jnp.eye(width, dtype=jnp.float32), lower=True
    )
    ncol = lax.axis_size("col")
    nrow = lax.axis_size("row")
    col_index = lax.axis_index("col")
    tile_mask = jnp.repeat(jnp.repeat(pattern[0], BS, axis=0), BS, axis=1).astype(jnp.float32)
    masked = panel[0] * tile_mask
    rows_dev = masked.shape[0]
    full_rows = lax.all_gather(masked, "col", axis=1, tiled=True)
    factor_rows = lax.dot_general(full_rows, inverse, contract, precision=highest)
    share = width // ncol
    own_cols = lax.dynamic_slice_in_dim(factor_rows, col_index * share, share, 1)
    cw_dev = contribution.shape[2]
    head_piece = lax.dynamic_slice_in_dim(factor_rows, col_index * cw_dev, cw_dev, 0)
    head_rows = from_root(head_piece, "row", 0)
    update = contribution[0] - lax.dot_general(factor_rows, head_rows, contract, precision=highest)
    blk = rows_dev // BS
    cap = max(2, blk // nrow)
    pblk = blk // 2
    blocks = update.reshape(blk, BS * cw_dev)
    target = route[0, :, 0]
    place = slot[0]
    order_ids = jnp.arange(blk, dtype=jnp.int32)
    earlier = (target[None, :] == target[:, None]) & (order_ids[None, :] < order_ids[:, None])
    rank = jnp.sum(earlier.astype(jnp.int32), axis=1)
    half = target // nrow
    target_row = target % nrow
    position = target_row * (2 * cap) + half * cap + rank
    slots_all = jnp.arange(nrow * 2 * cap, dtype=jnp.int32)
    onehot = (position[None, :] == slots_all[:, None]).astype(jnp.float32)
    packed = jnp.dot(onehot, blocks, precision=highest).reshape(nrow, 2, cap, BS * cw_dev)
    labels = jnp.dot(onehot, (place + 1).astype(jnp.float32), precision=highest).reshape(
        nrow, 2, cap
    )
    mine = lax.axis_index("cube") % 2
    got, got_labels = (
        lax.all_to_all(packed, "row", split_axis=0, concat_axis=0, tiled=True),
        lax.all_to_all(labels, "row", split_axis=0, concat_axis=0, tiled=True),
    )
    keep = lax.dynamic_index_in_dim(got, mine, 1, keepdims=False)
    keep_labels = lax.dynamic_index_in_dim(got_labels, mine, 1, keepdims=False)
    other = lax.dynamic_index_in_dim(got, 1 - mine, 1, keepdims=False)
    other_labels = lax.dynamic_index_in_dim(got_labels, 1 - mine, 1, keepdims=False)
    back, back_labels = partner((other, other_labels), "cube", 0)
    incoming = jnp.concatenate([keep, back], axis=0).reshape(-1, BS * cw_dev)
    tags = jnp.concatenate([keep_labels, back_labels], axis=0).reshape(-1)
    wanted = jnp.arange(1, pblk + 1, dtype=jnp.float32)
    select = (tags[None, :] == wanted[:, None]).astype(jnp.float32)
    assembled = jnp.dot(select, incoming, precision=highest).reshape(pblk * BS, cw_dev)
    rows_here = diag_block.shape[1]
    diag_rows = lax.dynamic_slice_in_dim(
        lower, lax.axis_index(("row", "col")) * rows_here, rows_here, 0
    )
    return (diag_rows[None], own_cols[None], assembled[None])


def solution(mesh):
    return jax.shard_map(
        on_device,
        mesh=mesh,
        in_specs=(
            P("cube", ("row", "col"), None),
            P("cube", "row", "col"),
            P("cube", "row", "col"),
            P("cube", "row", "col"),
            P("cube", "row", None),
            P("cube", "row"),
        ),
        out_specs=(
            P("cube", ("row", "col"), None),
            P("cube", "row", "col"),
            P("cube", "row", "col"),
        ),
        check_vma=False,
    )
```

profile of v0, /device:TPU:0, one launch (start us, length us, event | category | flops | bytes accessed | tf_op | source)
XLA Modules:
  0.0 502.8 jit_solution(4709540944532990716)
XLA Ops:
  7.2 1.7 copy.14
  9.0 0.7 convert_bitcast_fusion.2
  9.7 4.2 bitcast_multiply_fusion
  14.8 0.8 iota_compare_fusion
  15.7 20.9 %all-gather.3.cloned.1.call-done = f32[1,512,512]{2,0,1:T(1,128)} async-done(((f32[1,64,512]{2,0,1:T(1,128)}), f32[1,512,512]{2,0,1:T(1,128)}) %all-gather.3.cloned.1.call-update) | async-done | bytes 1048592 | tf_op jit(solution)/shard_map/all_gather | solution.py:23
  36.6 2.3 copy.15
  38.9 1.4 fusion.10
  40.4 11.7 %cholesky.104 = f32[128,128]{1,0:T(8,128)S(1)} custom-call(f32[128,128]{1,0:T(8,128)S(1)} %cholesky.266), custom_call_target="Cholesky" | custom-call | tf_op jit(solution)/shard_map/jit(cholesky)/cholesky | solution.py:25
  52.3 9.8 %custom-call.31 = f32[1,128,128]{1,2,0:T(8,128)S(1)} custom-call(f32[1,128,128]{2,1,0:T(8,128)S(1)} %get-tuple-element.34), custom_call_target="InvertDiagBlocksLowerTriangular" | custom-call | tf_op jit(solution)/shard_map/jit(cholesky)/cholesky | solution.py:25
  62.7 11.7 %cholesky.217 = f32[128,128]{1,0:T(8,128)S(1)} custom-call(f32[128,128]{1,0:T(8,128)S(1)} %cholesky.270), custom_call_target="Cholesky" | custom-call | tf_op jit(solution)/shard_map/jit(cholesky)/cholesky | solution.py:25
  74.5 10.0 %custom-call.32 = f32[1,128,128]{1,2,0:T(8,128)S(1)} custom-call(f32[1,128,128]{2,1,0:T(8,128)S(1)} %get-tuple-element.31), custom_call_target="InvertDiagBlocksLowerTriangular" | custom-call | tf_op jit(solution)/shard_map/jit(cholesky)/cholesky | solution.py:25
  85.2 11.7 %cholesky.238 = f32[128,128]{1,0:T(8,128)S(1)} custom-call(f32[128,128]{1,0:T(8,128)S(1)} %cholesky.275), custom_call_target="Cholesky" | custom-call | tf_op jit(solution)/shard_map/jit(cholesky)/cholesky | solution.py:25
  97.0 9.8 %custom-call.33 = f32[1,128,128]{1,2,0:T(8,128)S(1)} custom-call(f32[1,128,128]{2,1,0:T(8,128)S(1)} %get-tuple-element.28), custom_call_target="InvertDiagBlocksLowerTriangular" | custom-call | tf_op jit(solution)/shard_map/jit(cholesky)/cholesky | solution.py:25
  107.4 11.7 %cholesky.255 = f32[128,128]{1,0:T(8,128)S(1)} custom-call(f32[128,128]{1,0:T(8,128)S(1)} %convolution_subtract_fusion.6), custom_call_target="Cholesky" | custom-call | tf_op jit(solution)/shard_map/jit(cholesky)/cholesky | solution.py:25
  119.1 0.6 compare_reduce_fusion.2
  121.0 0.6 compare_reduce_fusion.1
  122.4 0.6 compare_reduce_fusion
  123.6 1.2 fusion.11
  124.9 10.9 %while.1 = (s32[]{:T(128)}, f32[512,512]{1,0:T(8,128)S(1)}, s32[4,2]{0,1:T(2,128)S(1)}, f32[4,128,128]{2,1,0:T(8,128)}, s32[]{:T(128)}) while((s32[]{:T(128)}, f32[512,512]{1,0:T(8,128)S(1)}, s32[4,2]{0,1:T(2,128)S(1)}, f32[4,128,128]{2,1,0:T(8,128)}, s32[]{:T(128)}) %tuple.34), condition=%wide.while_cond, body=%wide.while_body.sunk | while | flops 2 | bytes 132205 | solution.py:26
  125.0 0.6 fusion.72
  125.6 2.1 bitcast_dynamic-update-slice_fusion.2
  127.7 0.6 fusion.72
  128.3 2.1 bitcast_dynamic-update-slice_fusion.2
  131.0 2.1 bitcast_dynamic-update-slice_fusion.2
  133.7 2.1 bitcast_dynamic-update-slice_fusion.2
  135.8 50.1 %custom-call.34 = f32[4,128,128]{1,2,0:T(8,128)S(1)} custom-call(f32[4,128,128]{2,1,0:T(8,128)} %get-tuple-element.10), custom_call_target="InvertDiagBlocksLowerTriangular" | custom-call | tf_op jit(solution)/shard_map/jit(_solve_triangular)/triangular_solve | solution.py:26
  185.9 1.1 fusion.22
  188.6 0.6 convolution_subtract_fusion.3
  189.7 32.8 %fusion.2 = f32[8192,512]{1,0:T(8,128)S(1)} fusion(f32[8192,512]{1,0:T(8,128)} %all-gather.5.cloned.1.call-done, f32[128,512]{1,0:T(8,128)S(1)} %fusion.34, f32[128,512]{1,0:T(8,128)S(1)} %fusion.35, f32[128,512]{1,0:T(8,128)S(1)} %fusion.37, f32[128,512]{1,0:T(8,128)S(1)} %fusion.22), kind=kOutput, calls=%fused_computation.18 | convolution fusion | flops 25770590208 | bytes 34603008 | tf_op jit(solution)/shard_map/dot_general | solution.py:36
  222.6 5.7 %copy-done = f32[8192,512]{1,0:T(8,128)} copy-done((f32[8192,512]{1,0:T(8,128)}, f32[8192,512]{1,0:T(8,128)S(1)}, u32[]{:S(2)}) %copy-start) | copy-done | bytes 16777240
  228.3 0.7 dynamic-slice_select_fusion
  229.0 23.4 %all-reduce.3.cloned.1.call-done = f32[128,512]{1,0:T(8,128)} async-done(((f32[128,512]{1,0:T(8,128)}), f32[128,512]{1,0:T(8,128)}) %all-reduce.3.cloned.1.call-update) | async-done | bytes 262160 | tf_op jit(solution)/shard_map/psum | solution.py:11
  252.5 18.0 %convolution_subtract_fusion = f32[8192,128]{1,0:T(8,128)} fusion(f32[8192,512]{1,0:T(8,128)} %copy-done, f32[128,512]{1,0:T(8,128)} %all-reduce.3.cloned.1.call-done, f32[1,8192,128]{2,1,0:T(8,128)} %param.9), kind=kOutput, calls=%fused_computation.2 | convolution fusion | flops 6443499520 | bytes 25427968 | tf_op jit(solution)/shard_map/dot_general | solution.py:42
  270.5 4.9 reshape.183
  275.5 8.8 %fusion = f32[2,2,32,16384]{3,2,1,0:T(8,128)} fusion(f32[64,16384,1,1]{1,0,2,3:T(8,128)} %reshape.183, s32[2,2,32]{2,1,0:T(2,128)S(1)} %multiply_add_fusion, s32[64]{0:T(128)S(1)} %fusion.54), kind=kOutput, calls=%fused_computation.4 | convolution fusion | flops 1610620928 | bytes 12583680 | tf_op jit(solution)/shard_map/dot_general | solution.py:57
  284.2 6.9 %all-to-all-start.1 = ((f32[2,2,32,16384]{3,2,1,0:T(8,128)}), f32[2,2,32,16384]{3,2,1,0:T(8,128)}, u32[]{:S(2)}, u32[]{:S(2)}) async-start(f32[2,2,32,16384]{3,2,1,0:T(8,128)} %fusion), calls=%async_computation.1 | async-start | bytes 16777216 | tf_op jit(solution)/shard_map/all_to_all | solution.py:63
  291.2 92.1 %all-to-all-done.1 = f32[2,2,32,16384]{3,2,1,0:T(8,128)} async-done(((f32[2,2,32,16384]{3,2,1,0:T(8,128)}), f32[2,2,32,16384]{3,2,1,0:T(8,128)}, u32[]{:S(2)}, u32[]{:S(2)}) %all-to-all-start.1) | async-done | bytes 8388640 | tf_op jit(solution)/shard_map/all_to_all | solution.py:63
  383.3 7.5 %dynamic-slice_bitcast_fusion.1 = (f32[2,32,16384]{2,1,0:T(8,128)}, f32[2,32,16384]{2,1,0:T(8,128)}) fusion(f32[2,2,32,16384]{3,2,1,0:T(8,128)} %all-to-all-done.1, s32[]{:T(128)S(6)} %select_n.63, s32[]{:T(128)S(6)} %select_n.64), kind=kLoop, calls=%fused_computation.8 | loop fusion | bytes 16777224 | tf_op jit(solution)/shard_map/jit(dynamic_index_in_dim)/squeeze | solution.py:66
  390.7 1.5 collective-permute-start.1
  392.2 0.9 fusion.32
  393.1 3.5 all-to-all-start
  396.6 3.7 all-to-all-done
  400.9 81.1 %collective-permute-done = f32[2,32]{1,0:T(2,128)S(1)} collective-permute-done((f32[2,32]{1,0:T(2,128)S(1)}, f32[2,32]{1,0:T(2,128)S(1)}, u32[]{:S(2)}, u32[]{:S(2)}) %collective-permute-start) | collective-permute-done | bytes 288 | tf_op jit(solution)/shard_map/ppermute | solution.py:17
  482.1 1.6 dynamic-slice_bitcast_fusion.3
  483.7 4.6 dynamic-slice_bitcast_fusion.2
  488.3 2.8 pad_maximum_fusion
  491.1 3.2 fusion.48
  494.3 1.5 broadcast_in_dim_reshape.4
  (53 shorter events, 7.5 us)
Async XLA Ops:
  7.2 29.4 %all-gather.3.cloned.1.call-start = ((), (), s32[]{:S(2)}) async-start(), calls=%async_computation.2 | async-start | bytes 1179648 | tf_op jit(solution)/shard_map/all_gather | solution.py:23
  8.9 180.8 %all-gather.5.cloned.1.call-start = ((), (), s32[]{:S(2)}) async-start(), calls=%async_computation.3 | async-start | bytes 20971520 | tf_op jit(solution)/shard_map/all_gather | solution.py:35
  13.9 0.7 copy-start.2
  14.0 238.5 %all-reduce.3.cloned.1.call-start = ((), (), s32[]{:S(2)}) async-start(), calls=%async_computation.4 | async-start | bytes 524288 | tf_op jit(solution)/shard_map/psum | solution.py:11
  222.6 5.7 %copy-start = (f32[8192,512]{1,0:T(8,128)}, f32[8192,512]{1,0:T(8,128)S(1)}, u32[]{:S(2)}) copy-start(f32[8192,512]{1,0:T(8,128)S(1)} %fusion.2) | copy-start | bytes 50331652
  284.2 99.0 %all-to-all-start.1 = ((f32[2,2,32,16384]{3,2,1,0:T(8,128)}), f32[2,2,32,16384]{3,2,1,0:T(8,128)}, u32[]{:S(2)}, u32[]{:S(2)}) async-start(f32[2,2,32,16384]{3,2,1,0:T(8,128)} %fusion), calls=%async_computation.1 | async-start | bytes 16777216 | tf_op jit(solution)/shard_map/all_to_all | solution.py:63
  291.2 101.0 %copy-start.3 = (s32[1,64]{1,0:T(1,128)S(1)}, s32[1,64]{1,0:T(1,128)}, u32[]{:S(2)}) copy-start(s32[1,64]{1,0:T(1,128)} %param.11) | copy-start | bytes 772
  390.7 97.6 %collective-permute-start.1 = (f32[2,32,16384]{2,1,0:T(8,128)}, f32[2,32,16384]{2,1,0:T(8,128)}, u32[]{:S(2)}, u32[]{:S(2)}) collective-permute-start(f32[2,32,16384]{2,1,0:T(8,128)} %get-tuple-element.24), channel_id=1, source_target_pairs={{0,8},{8,0},{16,24},{24,16},{1,9},{9,1},{17,25},{25,17},{2,10},{10... | collective-permute-start | bytes 12582920 | tf_op jit(solution)/shard_map/ppermute | solution.py:17
  393.1 7.2 %all-to-all-start = ((f32[2,2,32]{2,1,0:T(2,128)}), f32[2,2,32]{2,1,0:T(2,128)S(1)}, u32[]{:S(2)}, u32[]{:S(2)}) async-start(f32[2,2,32]{2,1,0:T(2,128)} %bitcast.23), calls=%async_computation | async-start | bytes 4096 | tf_op jit(solution)/shard_map/all_to_all | solution.py:64
  400.4 81.7 %collective-permute-start = (f32[2,32]{1,0:T(2,128)S(1)}, f32[2,32]{1,0:T(2,128)S(1)}, u32[]{:S(2)}, u32[]{:S(2)}) collective-permute-start(f32[2,32]{1,0:T(2,128)S(1)} %bitcast.91), channel_id=1, source_target_pairs={{0,8},{8,0},{16,24},{24,16},{1,9},{9,1},{17,25},{25,17},{2,10},{10... | collective-permute-start | bytes 776 | tf_op jit(solution)/shard_map/ppermute | solution.py:17
  483.7 4.6 copy-start.1
Sparse Core Ops, SparseCore 0:
  10.4 26.0 all-gather.2
  38.7 108.2 all-gather.4
  229.1 23.2 all-reduce.2
where the time goes:
time: 513 us; the launch traced here: 503 us
  waiting for transfers between devices  221 us (43%)
  other arithmetic  141 us (27%)
  matrix products  69.4 us (14%)
  local copies, waits for them, and re-layouts  41.6 us (8%)
  between operations  17.1 us (3%)
  starting transfers between devices  12.6 us (2%)
    all_to_all x1, waiting for transfers between devices, on_device(): lax.all_to_all(packed, 'row', split_axis=0, concat_axis=0, tiled=True)  92.1 us
    ppermute x2, waiting for transfers between devices, partner(): return lax.ppermute(value, axis, pairs)  81.1 us
    another operation x14, other arithmetic, on_device(): lower = jnp.linalg.cholesky(whole)  78.6 us
    another operation x3, other arithmetic, on_device(): jax.scipy.linalg.solve_triangular(lower, jnp.eye(width, dtype=jnp.float32...  51.3 us
    dot_general x1, matrix products, on_device(): lax.dot_general(full_rows, inverse, contract, precision=highest)  32.8 us
    psum x1, waiting for transfers between devices, from_root(): return lax.psum(jnp.where(mine, value, jnp.zeros_like(value)), axis)  23.4 us
    all_gather x1, waiting for transfers between devices, on_device(): whole = lax.all_gather(diag_block, ('row', 'col'), axis=1, tiled=True)[0]  20.9 us
    dot_general x1, matrix products, on_device(): lax.dot_general(factor_rows, head_rows, contract, precision=highest)  18 us
  transfers between devices with their start and end apart: 7, of which 5 were waited for; matrix products, arithmetic and copies ran while one was open for 33% of the time, Pallas kernels for 0%

commit v1 on v0

--- a/solution.py
+++ b/solution.py
@@ -1,9 +1,382 @@
+import functools
+
 import jax
 import jax.numpy as jnp
 from jax import lax
+from jax.experimental import pallas as pl
+from jax.experimental.pallas import tpu as pltpu
 from jax.sharding import PartitionSpec as P
 
 BS = 128
+HIGHEST = lax.Precision.HIGHEST
+NT = (((1,), (1,)), ((), ()))
+ANY = pl.BlockSpec(memory_space=pl.ANY)
+VMEM = pl.BlockSpec(memory_space=pltpu.VMEM)
+MESH = pl.DeviceIdType.MESH
+
+
+def remote(src, dst, send, recv, device):
+    return pltpu.make_async_remote_copy(
+        src_ref=src, dst_ref=dst, send_sem=send, recv_sem=recv,
+        device_id=device, device_id_type=MESH,
+    )
+
+
+def factor_block(s_ref, x_ref):
+    n = BS
+    sub = lax.broadcasted_iota(jnp.int32, (n, n), 0)
+    lane = lax.broadcasted_iota(jnp.int32, (n, n), 1)
+    x_ref[...] = (sub == lane).astype(jnp.float32)
+    step = 32
+    for lo in range(0, n, step):
+        rows = n - lo
+        lane_r = lax.broadcasted_iota(jnp.int32, (rows, n), 1)
+        sub_c = lax.broadcasted_iota(jnp.int32, (rows, 1), 0) + lo
+        lane_1 = lax.broadcasted_iota(jnp.int32, (1, n), 1)
+
+        def body(j, carry):
+            s = s_ref[pl.ds(lo, rows), :]
+            x = x_ref[pl.ds(lo, rows), :]
+            row_s = s_ref[pl.ds(j, 1), :]
+            row_x = x_ref[pl.ds(j, 1), :]
+            col = jnp.sum(jnp.where(lane_r == j, s, 0.0), axis=1, keepdims=True)
+            pivot = jnp.sum(jnp.where(lane_1 == j, row_s, 0.0), axis=1, keepdims=True)
+            scale = 1.0 / pivot
+            col = jnp.where(sub_c > j, col, 0.0)
+            s_ref[pl.ds(lo, rows), :] = s - col * (row_s * scale)
+            x_ref[pl.ds(lo, rows), :] = x - col * (row_x * scale)
+            return carry
+
+        lax.fori_loop(lo, lo + step, body, 0)
+
+
+def cholesky_inverse(a_ref, inv_ref, s_ref, x_ref, between):
+    width = a_ref.shape[0]
+    sub = lax.broadcasted_iota(jnp.int32, (BS, BS), 0)
+    lane = lax.broadcasted_iota(jnp.int32, (BS, BS), 1)
+    inv_ref[...] = jnp.zeros_like(inv_ref)
+    for p in range(width // BS):
+        o, e = p * BS, (p + 1) * BS
+        s_ref[...] = a_ref[o:e, o:e]
+        factor_block(s_ref, x_ref)
+        s = s_ref[...]
+        d = jnp.sum(jnp.where(lane == sub, s, 0.0), axis=1, keepdims=True)
+        rs = 1.0 / jnp.sqrt(d)
+        low = jnp.transpose(jnp.where(lane >= sub, s, 0.0) * rs)
+        x = x_ref[...] * rs
+        a_ref[o:e, o:e] = low
+        inv_ref[o:e, o:e] = x
+        if e < width:
+            below = lax.dot_general(a_ref[e:, o:e], x, NT, precision=HIGHEST)
+            a_ref[e:, o:e] = below
+            a_ref[e:, e:] = a_ref[e:, e:] - lax.dot_general(below, below, NT, precision=HIGHEST)
+            a_ref[o:e, e:] = jnp.zeros((BS, width - e), jnp.float32)
+        if p > 0:
+            part = jnp.dot(a_ref[o:e, :o], inv_ref[:o, :o], precision=HIGHEST)
+            inv_ref[o:e, :o] = -jnp.dot(x, part, precision=HIGHEST)
+        between(p)
+
+
+def gather_kernel(chunks, diag_ref, panel_ref, g0_ref, g1_ref, g2_ref, l_ref, v_ref,
+                  a_ref, inv_ref, s_ref, x_ref, h_ref, hc_ref, w_ref,
+                  dsend, drecv, xsend, xrecv, fsend, frecv, psend, precv, hsend, hrecv, lsem):
+    r, c = lax.axis_index("row"), lax.axis_index("col")
+    y = 1 - r
+    c1 = c + 1 - 2 * (c % 2)
+    c2 = (c + 2) % 4
+    c3 = (c1 + 2) % 4
+    order = (c, c1, c2, c3)
+    ndiag = diag_ref.shape[0]
+    rows = panel_ref.shape[0] // chunks
+
+    barrier = pltpu.get_barrier_semaphore()
+    for rr in (r, y):
+        for cc in order:
+            if not (rr is r and cc is c):
+                pl.semaphore_signal(barrier, inc=1, device_id={"row": rr, "col": cc}, device_id_type=MESH)
+    pl.semaphore_wait(barrier, 7)
+
+    def spot(rr, cc):
+        return a_ref.at[pl.ds(pl.multiple_of((rr * 4 + cc) * ndiag, ndiag), ndiag)]
+
+    def diag_copy(k, src, rr, cc, device):
+        return remote(src, spot(rr, cc), dsend.at[k], drecv.at[k], device)
+
+    first = diag_copy(0, diag_ref, r, c, {"row": r, "col": c2})
+    first.start()
+    across = [
+        remote(panel_ref.at[pl.ds(i * rows, rows)], g1_ref.at[pl.ds(i * rows, rows)],
+               xsend.at[i], xrecv.at[i], {"row": r, "col": c2})
+        for i in range(chunks)
+    ]
+    onward = [
+        remote(g1_ref.at[pl.ds(i * rows, rows)], g2_ref.at[pl.ds(i * rows, rows)],
+               fsend.at[i], frecv.at[i], {"row": r, "col": c1})
+        for i in range(chunks)
+    ]
+    own = remote(panel_ref, g0_ref, psend, precv, {"row": r, "col": c1})
+    for copy in across:
+        copy.start()
+    second = [diag_copy(1, diag_ref, r, c, {"row": y, "col": c})]
+    second[0].start()
+    a_ref[pl.ds(pl.multiple_of((r * 4 + c) * ndiag, ndiag), ndiag), :] = diag_ref[...]
+    first.wait_recv()
+    second.append(diag_copy(2, spot(r, c2), r, c2, {"row": y, "col": c}))
+    second[1].start()
+    third = [
+        diag_copy(3, diag_ref, r, c, {"row": r, "col": c1}),
+        diag_copy(4, spot(r, c2), r, c2, {"row": r, "col": c1}),
+    ]
+    for copy in third:
+        copy.start()
+    for k, copy in enumerate(second):
+        copy.wait_recv()
+    third.append(diag_copy(5, spot(y, c), y, c, {"row": r, "col": c1}))
+    third.append(diag_copy(6, spot(y, c2), y, c2, {"row": r, "col": c1}))
+    for copy in third[2:]:
+        copy.start()
+    for copy in third:
+        copy.wait_recv()
+    for copy in [first] + second + third:
+        copy.wait_send()
+    own.start()
+
+    def between(p):
+        across[p].wait_recv()
+        onward[p].start()
+
+    cholesky_inverse(a_ref, inv_ref, s_ref, x_ref, between)
+    l_ref[...] = a_ref[pl.ds(pl.multiple_of((r * 4 + c) * ndiag, ndiag), ndiag), :]
+
+    own.wait_recv()
+    onward[0].wait_recv()
+    head = remote(h_ref, h_ref, hsend, hrecv, {"row": y, "col": c})
+
+    @pl.when(r == 0)
+    def _():
+        window = pl.ds(pl.multiple_of(c * BS, BS), BS)
+        loads = [
+            pltpu.make_async_copy(src.at[window], h_ref.at[j], lsem.at[j])
+            for j, src in enumerate((panel_ref, g0_ref, g1_ref, g2_ref))
+        ]
+        for copy in loads:
+            copy.start()
+        for copy in loads:
+            copy.wait()
+        head.start()
+        head.wait_send()
+
+    @pl.when(r == 1)
+    def _():
+        head.wait_recv()
+
+    for i in range(4, chunks):
+        across[i].wait_recv()
+        onward[i].start()
+    for j, k in enumerate(order):
+        hc_ref[:, pl.ds(pl.multiple_of(k * BS, BS), BS)] = h_ref[j]
+    factor_head = lax.dot_general(hc_ref[...], inv_ref[...], NT, precision=HIGHEST)
+    w_ref[pl.ds(BS, BS), :] = jnp.dot(factor_head, inv_ref[...], precision=HIGHEST)
+    w_ref[pl.ds(0, BS), :] = inv_ref[pl.ds(pl.multiple_of(c * BS, BS), BS), :]
+    for j, k in enumerate(order):
+        v_ref[j] = w_ref[:, pl.ds(pl.multiple_of(k * BS, BS), BS)]
+    for i in range(1, chunks):
+        onward[i].wait_recv()
+    for i in range(chunks):
+        across[i].wait_send()
+        onward[i].wait_send()
+    own.wait_send()
+
+
+def gather_and_factor(diag, masked):
+    chunks = 8
+    rows, share = masked.shape
+    ndiag, width = diag.shape
+    piece = jax.ShapeDtypeStruct((rows, share), jnp.float32)
+    return pl.pallas_call(
+        functools.partial(gather_kernel, chunks),
+        out_shape=(
+            piece, piece, piece,
+            jax.ShapeDtypeStruct((ndiag, width), jnp.float32),
+            jax.ShapeDtypeStruct((4, 2 * BS, BS), jnp.float32),
+        ),
+        in_specs=[VMEM, ANY],
+        out_specs=(ANY, ANY, ANY, VMEM, VMEM),
+        scratch_shapes=[
+            pltpu.VMEM((width, width), jnp.float32),
+            pltpu.VMEM((width, width), jnp.float32),
+            pltpu.VMEM((BS, BS), jnp.float32),
+            pltpu.VMEM((BS, BS), jnp.float32),
+            pltpu.VMEM((4, BS, BS), jnp.float32),
+            pltpu.VMEM((BS, width), jnp.float32),
+            pltpu.VMEM((2 * BS, width), jnp.float32),
+            pltpu.SemaphoreType.DMA((7,)),
+            pltpu.SemaphoreType.DMA((7,)),
+            pltpu.SemaphoreType.DMA((chunks,)),
+            pltpu.SemaphoreType.DMA((chunks,)),
+            pltpu.SemaphoreType.DMA((chunks,)),
+            pltpu.SemaphoreType.DMA((chunks,)),
+            pltpu.SemaphoreType.DMA,
+            pltpu.SemaphoreType.DMA,
+            pltpu.SemaphoreType.DMA,
+            pltpu.SemaphoreType.DMA,
+            pltpu.SemaphoreType.DMA((4,)),
+        ],
+        compiler_params=pltpu.CompilerParams(collective_id=0, has_side_effects=True),
+        name="gather_factor",
+    )(diag, masked)
+
+
+def split(value):
+    high = value.astype(jnp.bfloat16)
+    return high, (value - high.astype(jnp.float32)).astype(jnp.bfloat16)
+
+
+def update_kernel(tile, goal_ref, own_ref, g0_ref, g1_ref, g2_ref, contribution_ref, v_ref,
+                  f_ref, t_ref, vh_ref, vl_ref):
+    step = pl.program_id(0)
+
+    @pl.when(step == 0)
+    def _():
+        t_ref[...] = jnp.zeros_like(t_ref)
+        for j in range(4):
+            high, low = split(v_ref[j])
+            vh_ref[:, j * BS:(j + 1) * BS] = high
+            vl_ref[:, j * BS:(j + 1) * BS] = low
+
+    full = jnp.concatenate([own_ref[...], g0_ref[...], g1_ref[...], g2_ref[...]], axis=1)
+    high, low = split(full)
+    dot = functools.partial(lax.dot_general, dimension_numbers=NT, preferred_element_type=jnp.float32)
+    out = dot(high, vh_ref[...]) + (dot(high, vl_ref[...]) + dot(low, vh_ref[...]))
+    f_ref[...] = out[:, :BS]
+    update = contribution_ref[...] - out[:, BS:]
+    for b in range(tile // BS):
+        goal = goal_ref[step * (tile // BS) + b]
+        t_ref[goal] = t_ref[goal] + update[b * BS:(b + 1) * BS]
+
+
+def update_and_pack(goal, masked, pieces, contribution, v, slots):
+    tile = 512
+    rows, share = masked.shape
+    block = pl.BlockSpec((tile, share), lambda i, g: (i, 0))
+    return pl.pallas_call(
+        functools.partial(update_kernel, tile),
+        out_shape=(
+            jax.ShapeDtypeStruct((rows, share), jnp.float32),
+            jax.ShapeDtypeStruct((slots, BS, share), jnp.float32),
+        ),
+        grid_spec=pltpu.PrefetchScalarGridSpec(
+            num_scalar_prefetch=1,
+            grid=(rows // tile,),
+            in_specs=[block] * 5 + [pl.BlockSpec(v.shape, lambda i, g: (0, 0, 0))],
+            out_specs=(block, pl.BlockSpec((slots, BS, share), lambda i, g: (0, 0, 0))),
+            scratch_shapes=[pltpu.VMEM((2 * BS, 4 * BS), jnp.bfloat16)] * 2,
+        ),
+        compiler_params=pltpu.CompilerParams(dimension_semantics=("arbitrary",)),
+        name="update_pack",
+    )(goal, masked, *pieces, contribution, v)
+
+
+def route_kernel(t_ref, out_ref, ra, rb, ra2, rb2, asend, arecv, bsend, brecv,
+                 a2send, a2recv, b2send, b2recv):
+    z, r = lax.axis_index("cube"), lax.axis_index("row")
+    m, y = z % 2, 1 - r
+    dev_y = {"row": y}
+    dev_z = {"cube": z + 1 - 2 * m}
+    barrier = pltpu.get_barrier_semaphore()
+    for device in (dev_y, dev_z):
+        pl.semaphore_signal(barrier, inc=1, device_id=device, device_id_type=MESH)
+    pl.semaphore_wait(barrier, 2)
+    half = t_ref.shape[1] // 2
+    n = 8
+    parts = half // n
+    over_a, over_b = {}, {}
+    for rel in range(2):
+        for k in range(parts):
+            h = (1 - m) if rel == 0 else m
+            over_a[rel, k] = remote(
+                t_ref.at[h * 2 + y, pl.ds(k * n, n)], ra.at[rel, pl.ds(k * n, n)],
+                asend.at[rel, k], arecv.at[rel, k], dev_y)
+            rr = y if rel == 0 else r
+            over_b[rel, k] = remote(
+                t_ref.at[(1 - m) * 2 + rr, pl.ds(half + k * n, n)], rb.at[rel, pl.ds(k * n, n)],
+                bsend.at[rel, k], brecv.at[rel, k], dev_z)
+            over_a[rel, k].start()
+            over_b[rel, k].start()
+    last = {}
+    for k in range(parts):
+        part = pl.ds(k * n, n)
+        other = pl.ds(half + k * n, n)
+        over_a[0, k].wait_recv()
+        ra[0, part] = ra[0, part] + t_ref[(1 - m) * 2 + r, part]
+        over_b[0, k].wait_recv()
+        rb[0, part] = rb[0, part] + t_ref[m * 2 + y, other]
+        last[0, k] = remote(ra.at[0, part], ra2.at[part], a2send.at[k], a2recv.at[k], dev_z)
+        last[1, k] = remote(rb.at[0, part], rb2.at[part], b2send.at[k], b2recv.at[k], dev_y)
+        last[0, k].start()
+        last[1, k].start()
+    for k in range(parts):
+        part = pl.ds(k * n, n)
+        other = pl.ds(half + k * n, n)
+        over_a[1, k].wait_recv()
+        out_ref[part] = t_ref[m * 2 + r, part] + ra[1, part]
+        over_b[1, k].wait_recv()
+        out_ref[other] = t_ref[m * 2 + r, other] + rb[1, part]
+    for k in range(parts):
+        part = pl.ds(k * n, n)
+        other = pl.ds(half + k * n, n)
+        last[0, k].wait_recv()
+        out_ref[part] = out_ref[part] + ra2[part]
+        last[1, k].wait_recv()
+        out_ref[other] = out_ref[other] + rb2[part]
+    for copy in list(over_a.values()) + list(over_b.values()) + list(last.values()):
+        copy.wait_send()
+
+
+def route_blocks(packed):
+    _, slots, rows, share = packed.shape
+    half = slots // 2
+    parts = half // 8
+    return pl.pallas_call(
+        route_kernel,
+        out_shape=jax.ShapeDtypeStruct((slots, rows, share), jnp.float32),
+        in_specs=[VMEM],
+        out_specs=VMEM,
+        scratch_shapes=[
+            pltpu.VMEM((2, half, rows, share), jnp.float32),
+            pltpu.VMEM((2, half, rows, share), jnp.float32),
+            pltpu.VMEM((half, rows, share), jnp.float32),
+            pltpu.VMEM((half, rows, share), jnp.float32),
+            pltpu.SemaphoreType.DMA((2, parts)),
+            pltpu.SemaphoreType.DMA((2, parts)),
+            pltpu.SemaphoreType.DMA((2, parts)),
+            pltpu.SemaphoreType.DMA((2, parts)),
+            pltpu.SemaphoreType.DMA((parts,)),
+            pltpu.SemaphoreType.DMA((parts,)),
+            pltpu.SemaphoreType.DMA((parts,)),
+            pltpu.SemaphoreType.DMA((parts,)),
+        ],
+        compiler_params=pltpu.CompilerParams(collective_id=1, has_side_effects=True),
+        name="route_blocks",
+    )(packed)
+
+
+def mask_panel(panel, pattern):
+    tile_mask = jnp.repeat(jnp.repeat(pattern[0], BS, axis=0), BS, axis=1).astype(jnp.float32)
+    return panel[0] * tile_mask
+
+
+def on_small(diag_block, panel, pattern, contribution, route, slot):
+    masked = mask_panel(panel, pattern)
+    blk = masked.shape[0] // BS
+    pblk = blk // 2
+    nrow = lax.axis_size("row")
+    goal = (route[0, :, 0] * pblk + slot[0]).astype(jnp.int32)
+    g0, g1, g2, lower, v = gather_and_factor(diag_block[0], masked)
+    factor, packed = update_and_pack(goal, masked, (g0, g1, g2), contribution[0], v, 2 * nrow * pblk)
+    share = masked.shape[1]
+    assembled = route_blocks(packed.reshape(2 * nrow, pblk, BS, share))
+    return (lower[None], factor[None], assembled.reshape(1, pblk * BS, share))
 
 
 def from_root(value, axis, root):
@@ -17,7 +390,7 @@
     return lax.ppermute(value, axis, pairs)
 
 
-def on_device(diag_block, panel, pattern, contribution, route, slot):
+def on_large(diag_block, panel, pattern, contribution, route, slot):
     highest = lax.Precision.HIGHEST
     contract = (((1,), (1,)), ((), ()))
     whole = lax.all_gather(diag_block, ("row", "col"), axis=1, tiled=True)[0]
@@ -81,8 +454,9 @@
 
 
 def solution(mesh):
+    small = mesh.shape["row"] == 2 and mesh.shape["col"] == 4
     return jax.shard_map(
-        on_device,
+        on_small if small else on_large,
         mesh=mesh,
         in_specs=(
             P("cube", ("row", "col"), None),

time: 513 us -> 211 us (0.41); the launches traced: 503 us -> 211 us
  waiting for transfers between devices: 221 us -> 0 us
  Pallas kernels: 0 us -> 200 us
  other arithmetic: 141 us -> 6.01 us
  matrix products: 69.4 us -> 0 us
  local copies, waits for them, and re-layouts: 41.6 us -> 3.78 us
  between operations: 17.1 us -> 0.66 us
  starting transfers between devices: 12.6 us -> 0 us
    pallas_call x0 -> x3, Pallas kernels: none -> 200 us  [the longest x1 102 us: gather_and_factor(): pl.pallas_call(functools.partial(gather_kernel, chunks), out_shape=(piece...]
    another operation x17 -> x0, other arithmetic: 130 us -> none  [the longest x14 78.6 us: on_device(): lower = jnp.linalg.cholesky(whole)]
    all_to_all x2 -> x0, waiting for transfers between devices: 95.8 us -> none  [the longest x1 92.1 us: on_device(): lax.all_to_all(packed, 'row', split_axis=0, concat_axis=0, tiled=True)]
    ppermute x2 -> x0, waiting for transfers between devices: 81.1 us -> none  [partner(): return lax.ppermute(value, axis, pairs)]
    dot_general x5 -> x0, matrix products: 63.7 us -> none  [the longest x1 32.8 us: on_device(): lax.dot_general(full_rows, inverse, contract, precision=highest)]
    psum x1 -> x0, waiting for transfers between devices: 23.4 us -> none  [from_root(): return lax.psum(jnp.where(mine, value, jnp.zeros_like(value)), axis)]
    all_gather x2 -> x0, waiting for transfers between devices: 20.9 us -> none  [the longest x1 20.9 us: on_device(): whole = lax.all_gather(diag_block, ('row', 'col'), axis=1, tiled=True)[0]]
    another operation x18 -> x0, local copies, waits for them, and re-layouts: 12.5 us -> none
  transfers between devices with their start and end apart: 7 -> 0, of which waited for: 5 -> 0; matrix products, arithmetic and copies ran while one was open for 33% -> 0% of each run, Pallas kernels for 0% -> 0%
where the time goes in v1:
time: 211 us
  Pallas kernels  200 us (95%)
  other arithmetic  6.01 us (3%)
  local copies, waits for them, and re-layouts  3.78 us (2%)
    pallas_call x1, Pallas kernels, gather_and_factor(): pl.pallas_call(functools.partial(gather_kernel, chunks), out_shape=(piece...  102 us
    pallas_call x1, Pallas kernels, route_blocks(): pl.pallas_call(route_kernel, out_shape=jax.ShapeDtypeStruct((slots, rows,...  75.6 us
    pallas_call x1, Pallas kernels, update_and_pack(): pl.pallas_call(functools.partial(update_kernel, tile), out_shape=(jax.Sha...  22.2 us

profile of v1, /device:TPU:0, one launch (start us, length us, event | category | flops | bytes accessed | tf_op | source)
XLA Modules:
  0.0 210.7 jit_solution(15373487909950430266)
XLA Ops:
  0.6 0.7 convert_bitcast_fusion
  1.3 1.2 bitcast_add_fusion.goal_ref
  2.5 0.1 broadcast_bitcast_fusion
  2.5 4.2 %bitcast_multiply_fusion.panel_ref.own_ref = f32[8192,128]{1,0:T(8,128)} fusion(f32[1,8192,128]{2,1,0:T(8,128)} %param.7, f32[8192]{0:T(1024)S(1)} %broadcast_bitcast_fusion), kind=kLoop, calls=%fused_computation | loop fusion | flops 1048576 | bytes 8421376 | tf_op jit(solution)/shard_map/mul | solution.py:366
  6.7 102.4 %gather_factor.1 = (f32[8192,128]{1,0:T(8,128)}, f32[8192,128]{1,0:T(8,128)}, f32[8192,128]{1,0:T(8,128)}, f32[64,512]{1,0:T(8,128)}, f32[4,256,128]{2,1,0:T(8,128)}) custom-call(f32[64,512]{1,0:T(8,128)} %bitcast.19, f32[8192,128]{1,0:T(8,128)} %bitcast_multiply_fusion.panel_ref.own_ref), custom_call_target="tpu_custom_call" | custom-call | tf_op jit(solution)/shard_map/gather_factor/pallas_call | solution.py:196
  109.1 22.2 %update_pack.1 = (f32[8192,128]{1,0:T(8,128)}, f32[128,128,128]{2,1,0:T(8,128)}) custom-call(s32[64]{0:T(128)} %bitcast_add_fusion.goal_ref, f32[8192,128]{1,0:T(8,128)} %bitcast_multiply_fusion.panel_ref.own_ref, f32[8192,128]{1,0:T(8,128)} %get-tuple-element.11.g0_ref, f32[8192,128]{1,0:T(8,128)} %get-tuple-element.12.g1_ref, ...), custom_call_target="tpu_custom_call" | custom-call | tf_op jit(solution)/shard_map/update_pack/pallas_call | solution.py:262
  131.4 0.0 copy-start
  131.4 75.6 %route_blocks.1 = f32[32,128,128]{2,1,0:T(8,128)} custom-call(f32[4,32,128,128]{3,2,1,0:T(8,128)} %bitcast.16), custom_call_target="tpu_custom_call" | custom-call | tf_op jit(solution)/shard_map/route_blocks/pallas_call | solution.py:340
  207.0 0.0 copy-done
  207.0 0.7 copy.11
  207.6 3.0 %copy.12 = f32[1,4096,128]{2,1,0:T(8,128)} copy(f32[1,4096,128]{2,1,0:T(8,128)} %bitcast.17) | data formatting | bytes 4194304
Async XLA Ops:
  131.4 75.6 %copy-start = (f32[64,512]{1,0:T(8,128)S(1)}, f32[64,512]{1,0:T(8,128)}, u32[]{:S(2)}) copy-start(f32[64,512]{1,0:T(8,128)} %get-tuple-element.10) | copy-start | bytes 393220

commit v2 on v1

--- a/solution.py
+++ b/solution.py
@@ -77,24 +77,28 @@
         between(p)
 
 
-def gather_kernel(chunks, diag_ref, panel_ref, g0_ref, g1_ref, g2_ref, l_ref, v_ref,
-                  a_ref, inv_ref, s_ref, x_ref, h_ref, hc_ref, w_ref,
-                  dsend, drecv, xsend, xrecv, fsend, frecv, psend, precv, hsend, hrecv, lsem):
+def gather_kernel(chunks, diag_ref, mask_ref, panel_ref, contribution_ref, f_ref, u_ref, l_ref,
+                  own, g0, g1, g2, contrib, a_ref, inv_ref, s_ref, x_ref, h_ref, hc_ref, w_ref,
+                  vh_ref, vl_ref, masks, head_masks, fs, us,
+                  dsend, drecv, xsend, xrecv, fsend, frecv, psend, precv, hsend, hrecv,
+                  msend, mrecv, lsem, isem, osem):
     r, c = lax.axis_index("row"), lax.axis_index("col")
     y = 1 - r
     c1 = c + 1 - 2 * (c % 2)
     c2 = (c + 2) % 4
     c3 = (c1 + 2) % 4
     order = (c, c1, c2, c3)
+    pieces = (own, g0, g1, g2)
     ndiag = diag_ref.shape[0]
     rows = panel_ref.shape[0] // chunks
-
+    to_x, to_core, to_row = {"col": c2}, {"col": c1}, {"row": y}
+
+    load_own = pltpu.make_async_copy(panel_ref, own, isem.at[0])
+    load_contrib = pltpu.make_async_copy(contribution_ref, contrib, isem.at[1])
     barrier = pltpu.get_barrier_semaphore()
-    for rr in (r, y):
-        for cc in order:
-            if not (rr is r and cc is c):
-                pl.semaphore_signal(barrier, inc=1, device_id={"row": rr, "col": cc}, device_id_type=MESH)
-    pl.semaphore_wait(barrier, 7)
+    for device in (to_x, to_core, to_row):
+        pl.semaphore_signal(barrier, inc=1, device_id=device, device_id_type=MESH)
+    pl.semaphore_wait(barrier, 3)
 
     def spot(rr, cc):
         return a_ref.at[pl.ds(pl.multiple_of((rr * 4 + cc) * ndiag, ndiag), ndiag)]
@@ -102,129 +106,201 @@
     def diag_copy(k, src, rr, cc, device):
         return remote(src, spot(rr, cc), dsend.at[k], drecv.at[k], device)
 
-    first = diag_copy(0, diag_ref, r, c, {"row": r, "col": c2})
+    def across(i):
+        part = pl.ds(pl.multiple_of(i * rows, rows), rows)
+        return remote(panel_ref.at[part], g1.at[part], xsend.at[i], xrecv.at[i], to_x)
+
+    def onward(i):
+        part = pl.ds(pl.multiple_of(i * rows, rows), rows)
+        return remote(g1.at[part], g2.at[part], fsend.at[i], frecv.at[i], to_core)
+
+    own_piece = remote(panel_ref, g0, psend, precv, to_core)
+    mask_x = remote(mask_ref, masks.at[2], msend.at[0], mrecv.at[0], to_x)
+    mask_core = remote(mask_ref, masks.at[1], msend.at[1], mrecv.at[1], to_core)
+    mask_on = remote(masks.at[2], masks.at[3], msend.at[2], mrecv.at[2], to_core)
+
+    first = diag_copy(0, diag_ref, r, c, to_x)
     first.start()
-    across = [
-        remote(panel_ref.at[pl.ds(i * rows, rows)], g1_ref.at[pl.ds(i * rows, rows)],
-               xsend.at[i], xrecv.at[i], {"row": r, "col": c2})
-        for i in range(chunks)
-    ]
-    onward = [
-        remote(g1_ref.at[pl.ds(i * rows, rows)], g2_ref.at[pl.ds(i * rows, rows)],
-               fsend.at[i], frecv.at[i], {"row": r, "col": c1})
-        for i in range(chunks)
-    ]
-    own = remote(panel_ref, g0_ref, psend, precv, {"row": r, "col": c1})
-    for copy in across:
-        copy.start()
-    second = [diag_copy(1, diag_ref, r, c, {"row": y, "col": c})]
+    mask_x.start()
+    for i in range(chunks):
+        across(i).start()
+    second = [diag_copy(1, diag_ref, r, c, to_row)]
     second[0].start()
+    mask_core.start()
+    load_own.start()
+    load_contrib.start()
     a_ref[pl.ds(pl.multiple_of((r * 4 + c) * ndiag, ndiag), ndiag), :] = diag_ref[...]
+    masks[0] = mask_ref[...]
     first.wait_recv()
-    second.append(diag_copy(2, spot(r, c2), r, c2, {"row": y, "col": c}))
+    second.append(diag_copy(2, spot(r, c2), r, c2, to_row))
     second[1].start()
     third = [
-        diag_copy(3, diag_ref, r, c, {"row": r, "col": c1}),
-        diag_copy(4, spot(r, c2), r, c2, {"row": r, "col": c1}),
+        diag_copy(3, diag_ref, r, c, to_core),
+        diag_copy(4, spot(r, c2), r, c2, to_core),
     ]
     for copy in third:
         copy.start()
-    for k, copy in enumerate(second):
+    mask_x.wait_recv()
+    mask_on.start()
+    for copy in second:
         copy.wait_recv()
-    third.append(diag_copy(5, spot(y, c), y, c, {"row": r, "col": c1}))
-    third.append(diag_copy(6, spot(y, c2), y, c2, {"row": r, "col": c1}))
+    third.append(diag_copy(5, spot(y, c), y, c, to_core))
+    third.append(diag_copy(6, spot(y, c2), y, c2, to_core))
     for copy in third[2:]:
         copy.start()
     for copy in third:
         copy.wait_recv()
     for copy in [first] + second + third:
         copy.wait_send()
-    own.start()
+    own_piece.start()
+
+    ahead = chunks // 2
 
     def between(p):
-        across[p].wait_recv()
-        onward[p].start()
+        for i in range(p * ahead // 4, (p + 1) * ahead // 4):
+            across(i).wait_recv()
+            onward(i).start()
 
     cholesky_inverse(a_ref, inv_ref, s_ref, x_ref, between)
     l_ref[...] = a_ref[pl.ds(pl.multiple_of((r * 4 + c) * ndiag, ndiag), ndiag), :]
 
-    own.wait_recv()
-    onward[0].wait_recv()
-    head = remote(h_ref, h_ref, hsend, hrecv, {"row": y, "col": c})
+    load_own.wait()
+    load_contrib.wait()
+    own_piece.wait_recv()
+    mask_core.wait_recv()
+    mask_on.wait_recv()
+    early = max(1, 4 * BS // rows)
+    for i in range(early):
+        onward(i).wait_recv()
+    head = remote(h_ref, h_ref, hsend.at[0], hrecv.at[0], to_row)
+    head_mask = remote(masks, head_masks, hsend.at[1], hrecv.at[1], to_row)
+    window = pl.ds(pl.multiple_of(c * BS, BS), BS)
 
     @pl.when(r == 0)
     def _():
-        window = pl.ds(pl.multiple_of(c * BS, BS), BS)
         loads = [
-            pltpu.make_async_copy(src.at[window], h_ref.at[j], lsem.at[j])
-            for j, src in enumerate((panel_ref, g0_ref, g1_ref, g2_ref))
+            pltpu.make_async_copy(piece.at[window], h_ref.at[j], lsem.at[j])
+            for j, piece in enumerate(pieces)
         ]
         for copy in loads:
             copy.start()
         for copy in loads:
             copy.wait()
         head.start()
+        head_mask.start()
+        for j, k in enumerate(order):
+            hc_ref[:, pl.ds(pl.multiple_of(k * BS, BS), BS)] = h_ref[j] * masks[j, pl.ds(c, 1), :]
         head.wait_send()
+        head_mask.wait_send()
 
     @pl.when(r == 1)
     def _():
         head.wait_recv()
-
-    for i in range(4, chunks):
-        across[i].wait_recv()
-        onward[i].start()
-    for j, k in enumerate(order):
-        hc_ref[:, pl.ds(pl.multiple_of(k * BS, BS), BS)] = h_ref[j]
+        head_mask.wait_recv()
+        for j, k in enumerate(order):
+            hc_ref[:, pl.ds(pl.multiple_of(k * BS, BS), BS)] = h_ref[j] * head_masks[j, pl.ds(c, 1), :]
+
     factor_head = lax.dot_general(hc_ref[...], inv_ref[...], NT, precision=HIGHEST)
     w_ref[pl.ds(BS, BS), :] = jnp.dot(factor_head, inv_ref[...], precision=HIGHEST)
     w_ref[pl.ds(0, BS), :] = inv_ref[pl.ds(pl.multiple_of(c * BS, BS), BS), :]
     for j, k in enumerate(order):
-        v_ref[j] = w_ref[:, pl.ds(pl.multiple_of(k * BS, BS), BS)]
-    for i in range(1, chunks):
-        onward[i].wait_recv()
+        high, low = split(jnp.transpose(w_ref[:, pl.ds(pl.multiple_of(k * BS, BS), BS)]))
+        vh_ref[j * BS:(j + 1) * BS, :] = high
+        vl_ref[j * BS:(j + 1) * BS, :] = low
+
+    def stores(i, buf):
+        part = pl.ds(pl.multiple_of(i * rows, rows), rows)
+        return (
+            pltpu.make_async_copy(fs.at[buf], f_ref.at[part], osem.at[0, buf]),
+            pltpu.make_async_copy(us.at[buf], u_ref.at[part], osem.at[1, buf]),
+        )
+
+    def compute(i):
+        buf = i % 2
+
+        @pl.when(i >= 2)
+        def _():
+            for copy in stores(i - 2, buf):
+                copy.wait()
+
+        start = pl.multiple_of(i * rows, rows)
+        blocks = []
+        for b in range(rows // BS):
+            part = pl.ds(pl.multiple_of(start + b * BS, BS), BS)
+            at = i * (rows // BS) + b
+            blocks.append(jnp.concatenate(
+                [piece[part, :] * masks[j, pl.ds(at, 1), :] for j, piece in enumerate(pieces)], axis=1))
+        high, low = split(jnp.concatenate(blocks, axis=0))
+        dot = functools.partial(jnp.dot, preferred_element_type=jnp.float32)
+        out = dot(high, vh_ref[...]) + (dot(high, vl_ref[...]) + dot(low, vh_ref[...]))
+        fs[buf] = out[:, :BS]
+        us[buf] = contrib[pl.ds(start, rows), :] - out[:, BS:]
+        for copy in stores(i, buf):
+            copy.start()
+
+    def step(i, carry):
+        @pl.when((i >= ahead) & (i < chunks))
+        def _():
+            across(i).wait_recv()
+            onward(i).start()
+
+        @pl.when(i > early)
+        def _():
+            onward(i - 1).wait_recv()
+
+        @pl.when(i > 0)
+        def _():
+            compute(i - 1)
+        return carry
+
+    lax.fori_loop(0, chunks + 1, step, 0)
+    for i in (chunks - 2, chunks - 1):
+        for copy in stores(i, i % 2):
+            copy.wait()
     for i in range(chunks):
-        across[i].wait_send()
-        onward[i].wait_send()
-    own.wait_send()
-
-
-def gather_and_factor(diag, masked):
-    chunks = 8
-    rows, share = masked.shape
+        across(i).wait_send()
+        onward(i).wait_send()
+    own_piece.wait_send()
+    for copy in (mask_x, mask_core, mask_on):
+        copy.wait_send()
+
+
+def gather_and_factor(diag, mask, panel, contribution):
+    chunks = 16
+    rows, share = panel.shape
+    tile = rows // chunks
     ndiag, width = diag.shape
     piece = jax.ShapeDtypeStruct((rows, share), jnp.float32)
+    whole = pltpu.VMEM((rows, share), jnp.float32)
+    square = pltpu.VMEM((width, width), jnp.float32)
+    block = pltpu.VMEM((BS, BS), jnp.float32)
+    sems = pltpu.SemaphoreType.DMA
     return pl.pallas_call(
         functools.partial(gather_kernel, chunks),
-        out_shape=(
-            piece, piece, piece,
-            jax.ShapeDtypeStruct((ndiag, width), jnp.float32),
-            jax.ShapeDtypeStruct((4, 2 * BS, BS), jnp.float32),
-        ),
-        in_specs=[VMEM, ANY],
-        out_specs=(ANY, ANY, ANY, VMEM, VMEM),
+        out_shape=(piece, piece, jax.ShapeDtypeStruct((ndiag, width), jnp.float32)),
+        in_specs=[VMEM, VMEM, ANY, ANY],
+        out_specs=(ANY, ANY, VMEM),
         scratch_shapes=[
-            pltpu.VMEM((width, width), jnp.float32),
-            pltpu.VMEM((width, width), jnp.float32),
-            pltpu.VMEM((BS, BS), jnp.float32),
-            pltpu.VMEM((BS, BS), jnp.float32),
+            whole, whole, whole, whole, whole,
+            square, square, block, block,
             pltpu.VMEM((4, BS, BS), jnp.float32),
             pltpu.VMEM((BS, width), jnp.float32),
             pltpu.VMEM((2 * BS, width), jnp.float32),
-            pltpu.SemaphoreType.DMA((7,)),
-            pltpu.SemaphoreType.DMA((7,)),
-            pltpu.SemaphoreType.DMA((chunks,)),
-            pltpu.SemaphoreType.DMA((chunks,)),
-            pltpu.SemaphoreType.DMA((chunks,)),
-            pltpu.SemaphoreType.DMA((chunks,)),
-            pltpu.SemaphoreType.DMA,
-            pltpu.SemaphoreType.DMA,
-            pltpu.SemaphoreType.DMA,
-            pltpu.SemaphoreType.DMA,
-            pltpu.SemaphoreType.DMA((4,)),
+            pltpu.VMEM((width, 2 * BS), jnp.bfloat16),
+            pltpu.VMEM((width, 2 * BS), jnp.bfloat16),
+            pltpu.VMEM((4,) + mask.shape, jnp.float32),
+            pltpu.VMEM((4,) + mask.shape, jnp.float32),
+            pltpu.VMEM((2, tile, share), jnp.float32),
+            pltpu.VMEM((2, tile, share), jnp.float32),
+            sems((7,)), sems((7,)),
+            sems((chunks,)), sems((chunks,)), sems((chunks,)), sems((chunks,)),
+            sems, sems, sems((2,)), sems((2,)), sems((3,)), sems((3,)),
+            sems((4,)), sems((2,)), sems((2, 2)),
         ],
-        compiler_params=pltpu.CompilerParams(collective_id=0, has_side_effects=True),
+        compiler_params=pltpu.CompilerParams(
+            collective_id=0, has_side_effects=True, vmem_limit_bytes=48 * 2**20),
         name="gather_factor",
-    )(diag, masked)
+    )(diag, mask, panel, contribution)
 
 
 def split(value):
@@ -232,49 +308,39 @@
     return high, (value - high.astype(jnp.float32)).astype(jnp.bfloat16)
 
 
-def update_kernel(tile, goal_ref, own_ref, g0_ref, g1_ref, g2_ref, contribution_ref, v_ref,
-                  f_ref, t_ref, vh_ref, vl_ref):
+def pack_kernel(tile, pblk, route_ref, slot_ref, f_in, u_ref, f_ref, t_ref):
     step = pl.program_id(0)
 
     @pl.when(step == 0)
     def _():
         t_ref[...] = jnp.zeros_like(t_ref)
-        for j in range(4):
-            high, low = split(v_ref[j])
-            vh_ref[:, j * BS:(j + 1) * BS] = high
-            vl_ref[:, j * BS:(j + 1) * BS] = low
-
-    full = jnp.concatenate([own_ref[...], g0_ref[...], g1_ref[...], g2_ref[...]], axis=1)
-    high, low = split(full)
-    dot = functools.partial(lax.dot_general, dimension_numbers=NT, preferred_element_type=jnp.float32)
-    out = dot(high, vh_ref[...]) + (dot(high, vl_ref[...]) + dot(low, vh_ref[...]))
-    f_ref[...] = out[:, :BS]
-    update = contribution_ref[...] - out[:, BS:]
+
+    f_ref[...] = f_in[...]
     for b in range(tile // BS):
-        goal = goal_ref[step * (tile // BS) + b]
-        t_ref[goal] = t_ref[goal] + update[b * BS:(b + 1) * BS]
-
-
-def update_and_pack(goal, masked, pieces, contribution, v, slots):
-    tile = 512
-    rows, share = masked.shape
-    block = pl.BlockSpec((tile, share), lambda i, g: (i, 0))
+        at = step * (tile // BS) + b
+        goal = route_ref[at] * pblk + slot_ref[at]
+        t_ref[goal] = t_ref[goal] + u_ref[b * BS:(b + 1) * BS, :]
+
+
+def pack_blocks(route, slot, factor, update, slots, pblk):
+    tile = 1024
+    rows, share = factor.shape
+    block = pl.BlockSpec((tile, share), lambda i, g, s: (i, 0))
     return pl.pallas_call(
-        functools.partial(update_kernel, tile),
+        functools.partial(pack_kernel, tile, pblk),
         out_shape=(
             jax.ShapeDtypeStruct((rows, share), jnp.float32),
             jax.ShapeDtypeStruct((slots, BS, share), jnp.float32),
         ),
         grid_spec=pltpu.PrefetchScalarGridSpec(
-            num_scalar_prefetch=1,
+            num_scalar_prefetch=2,
             grid=(rows // tile,),
-            in_specs=[block] * 5 + [pl.BlockSpec(v.shape, lambda i, g: (0, 0, 0))],
-            out_specs=(block, pl.BlockSpec((slots, BS, share), lambda i, g: (0, 0, 0))),
-            scratch_shapes=[pltpu.VMEM((2 * BS, 4 * BS), jnp.bfloat16)] * 2,
+            in_specs=[block] * 2,
+            out_specs=(block, pl.BlockSpec((slots, BS, share), lambda i, g, s: (0, 0, 0))),
         ),
         compiler_params=pltpu.CompilerParams(dimension_semantics=("arbitrary",)),
-        name="update_pack",
-    )(goal, masked, *pieces, contribution, v)
+        name="pack_blocks",
+    )(route, slot, factor, update)
 
 
 def route_kernel(t_ref, out_ref, ra, rb, ra2, rb2, asend, arecv, bsend, brecv,
@@ -361,20 +427,14 @@
     )(packed)
 
 
-def mask_panel(panel, pattern):
-    tile_mask = jnp.repeat(jnp.repeat(pattern[0], BS, axis=0), BS, axis=1).astype(jnp.float32)
-    return panel[0] * tile_mask
-
-
 def on_small(diag_block, panel, pattern, contribution, route, slot):
-    masked = mask_panel(panel, pattern)
-    blk = masked.shape[0] // BS
+    rows, share = panel.shape[1:]
+    blk = rows // BS
     pblk = blk // 2
     nrow = lax.axis_size("row")
-    goal = (route[0, :, 0] * pblk + slot[0]).astype(jnp.int32)
-    g0, g1, g2, lower, v = gather_and_factor(diag_block[0], masked)
-    factor, packed = update_and_pack(goal, masked, (g0, g1, g2), contribution[0], v, 2 * nrow * pblk)
-    share = masked.shape[1]
+    mask = jnp.broadcast_to(pattern[0].astype(jnp.float32), (blk, share))
+    factor, update, lower = gather_and_factor(diag_block[0], mask, panel[0], contribution[0])
+    factor, packed = pack_blocks(route[0, :, 0], slot[0], factor, update, 2 * nrow * pblk, pblk)
     assembled = route_blocks(packed.reshape(2 * nrow, pblk, BS, share))
     return (lower[None], factor[None], assembled.reshape(1, pblk * BS, share))
 

time: 211 us -> 197 us (0.934)
  Pallas kernels: 200 us -> 189 us
  other arithmetic: 6.01 us -> 0.66 us
  local copies, waits for them, and re-layouts: 3.78 us -> 6.61 us
    pallas_call x1, Pallas kernels: 22.2 us -> 11.2 us  [pack_blocks(): pl.pallas_call(functools.partial(pack_kernel, tile, pblk), out_shape=(jax...]
    mul x1 -> x0, other arithmetic: 4.16 us -> none  [mask_panel(): return panel[0] * tile_mask]
    unnamed x4 -> x6, local copies, waits for them, and re-layouts: 3.71 us -> 6.54 us
where the time goes in v2:
time: 197 us
  Pallas kernels  189 us (96%)
  local copies, waits for them, and re-layouts  6.61 us (3%)
    pallas_call x1, Pallas kernels, gather_and_factor(): pl.pallas_call(functools.partial(gather_kernel, chunks), out_shape=(piece...  101 us
    pallas_call x1, Pallas kernels, route_blocks(): pl.pallas_call(route_kernel, out_shape=jax.ShapeDtypeStruct((slots, rows,...  76.5 us
    pallas_call x1, Pallas kernels, pack_blocks(): pl.pallas_call(functools.partial(pack_kernel, tile, pblk), out_shape=(jax...  11.2 us
    unnamed x6, local copies, waits for them, and re-layouts  6.54 us

profile of v2, /device:TPU:0, one launch (start us, length us, event | category | flops | bytes accessed | tf_op | source)
XLA Modules:
  0.0 196.8 jit_solution(13557221075943454767)
XLA Ops:
  0.6 0.7 convert_bitcast_fusion
  1.3 0.1 broadcast_in_dim.11.mask_ref
  1.4 0.0 copy-start.1
  1.4 0.9 copy-done.1
  2.3 101.2 %gather_factor.1 = (f32[8192,128]{1,0:T(8,128)S(1)}, f32[8192,128]{1,0:T(8,128)}, f32[64,512]{1,0:T(8,128)S(1)}) custom-call(f32[64,512]{1,0:T(8,128)S(1)} %bitcast.11, f32[64,128]{1,0:T(8,128)S(1)} %broadcast_in_dim.11.mask_ref, f32[8192,128]{1,0:T(8,128)} %bitcast.15, f32[8192,128]{1,0:T(8,128)} %bitcast.16), custom_call_target="tpu_custom_call" | custom-call | tf_op jit(solution)/shard_map/gather_factor/pallas_call | solution.py:278
  103.4 0.0 copy-start
  103.4 1.9 copy-done
  105.4 11.2 %pack_blocks.1 = (f32[8192,128]{1,0:T(8,128)}, f32[128,128,128]{2,1,0:T(8,128)}) custom-call(s32[64]{0:T(128)} %bitcast.17, s32[64]{0:T(128)} %bitcast.18, f32[8192,128]{1,0:T(8,128)} %copy-done, f32[8192,128]{1,0:T(8,128)} %get-tuple-element.10.u_ref), custom_call_target="tpu_custom_call" | custom-call | tf_op jit(solution)/shard_map/pack_blocks/pallas_call | solution.py:329
  116.6 76.5 %route_blocks.1 = f32[32,128,128]{2,1,0:T(8,128)} custom-call(f32[4,32,128,128]{3,2,1,0:T(8,128)} %bitcast.13), custom_call_target="tpu_custom_call" | custom-call | tf_op jit(solution)/shard_map/route_blocks/pallas_call | solution.py:406
  193.1 0.7 copy.11
  193.8 3.0 %copy.12 = f32[1,4096,128]{2,1,0:T(8,128)} copy(f32[1,4096,128]{2,1,0:T(8,128)} %bitcast.14) | data formatting | bytes 4194304
Async XLA Ops:
  1.4 0.9 copy-start.1
  103.4 1.9 copy-start

commit v3 on v2

--- a/solution.py
+++ b/solution.py
@@ -12,6 +12,7 @@
 NT = (((1,), (1,)), ((), ()))
 ANY = pl.BlockSpec(memory_space=pl.ANY)
 VMEM = pl.BlockSpec(memory_space=pltpu.VMEM)
+SMEM = pl.BlockSpec(memory_space=pltpu.SMEM)
 MESH = pl.DeviceIdType.MESH
 
 
@@ -77,11 +78,14 @@
         between(p)
 
 
-def gather_kernel(chunks, diag_ref, mask_ref, panel_ref, contribution_ref, f_ref, u_ref, l_ref,
+def gather_kernel(chunks, prev_ref, prev_on, last_ref, last_on, diag_ref, mask_ref, panel_ref, contribution_ref, f_ref, out_ref, l_ref,
                   own, g0, g1, g2, contrib, a_ref, inv_ref, s_ref, x_ref, h_ref, hc_ref, w_ref,
-                  vh_ref, vl_ref, masks, head_masks, fs, us,
+                  vh_ref, vl_ref, masks, head_masks, fs, t_ref, ra, rb, ra2, rb2,
                   dsend, drecv, xsend, xrecv, fsend, frecv, psend, precv, hsend, hrecv,
-                  msend, mrecv, lsem, isem, osem):
+                  msend, mrecv, lsem, isem, osem,
+                  asend, arecv, bsend, brecv, a2send, a2recv, b2send, b2recv):
+    z = lax.axis_index("cube")
+    m = z % 2
     r, c = lax.axis_index("row"), lax.axis_index("col")
     y = 1 - r
     c1 = c + 1 - 2 * (c % 2)
@@ -96,9 +100,10 @@
     load_own = pltpu.make_async_copy(panel_ref, own, isem.at[0])
     load_contrib = pltpu.make_async_copy(contribution_ref, contrib, isem.at[1])
     barrier = pltpu.get_barrier_semaphore()
-    for device in (to_x, to_core, to_row):
+    to_cube = {"cube": z + 1 - 2 * m}
+    for device in (to_x, to_core, to_row, to_cube):
         pl.semaphore_signal(barrier, inc=1, device_id=device, device_id_type=MESH)
-    pl.semaphore_wait(barrier, 3)
+    pl.semaphore_wait(barrier, 4)
 
     def spot(rr, cc):
         return a_ref.at[pl.ds(pl.multiple_of((rr * 4 + cc) * ndiag, ndiag), ndiag)]
@@ -210,10 +215,7 @@
 
     def stores(i, buf):
         part = pl.ds(pl.multiple_of(i * rows, rows), rows)
-        return (
-            pltpu.make_async_copy(fs.at[buf], f_ref.at[part], osem.at[0, buf]),
-            pltpu.make_async_copy(us.at[buf], u_ref.at[part], osem.at[1, buf]),
-        )
+        return (pltpu.make_async_copy(fs.at[buf], f_ref.at[part], osem.at[buf]),)
 
     def compute(i):
         buf = i % 2
@@ -234,9 +236,12 @@
         dot = functools.partial(jnp.dot, preferred_element_type=jnp.float32)
         out = dot(high, vh_ref[...]) + (dot(high, vl_ref[...]) + dot(low, vh_ref[...]))
         fs[buf] = out[:, :BS]
-        us[buf] = contrib[pl.ds(start, rows), :] - out[:, BS:]
         for copy in stores(i, buf):
             copy.start()
+        for b in range(rows // BS):
+            at = i * (rows // BS) + b
+            update = contrib[at] - out[b * BS:(b + 1) * BS, BS:]
+            contrib[at] = update + prev_on[at] * contrib[prev_ref[at]]
 
     def step(i, carry):
         @pl.when((i >= ahead) & (i < chunks))
@@ -254,6 +259,18 @@
         return carry
 
     lax.fori_loop(0, chunks + 1, step, 0)
+    slots = out_ref.shape[0]
+
+    def fill(h, rr, begin, end):
+        def body(k, carry):
+            name = (h * 2 + rr) * slots + k
+            t_ref[h * 2 + rr, k] = contrib[last_ref[name]] * last_on[name]
+            return carry
+
+        lax.fori_loop(begin, end, body, 0)
+
+    route_slots(m, r, y, to_row, to_cube, fill, t_ref, out_ref, ra, rb, ra2, rb2,
+                asend, arecv, bsend, brecv, a2send, a2recv, b2send, b2recv)
     for i in (chunks - 2, chunks - 1):
         for copy in stores(i, i % 2):
             copy.wait()
@@ -265,10 +282,12 @@
         copy.wait_send()
 
 
-def gather_and_factor(diag, mask, panel, contribution):
+def factor_and_route(chains, diag, mask, panel, contribution, pblk):
     chunks = 16
     rows, share = panel.shape
     tile = rows // chunks
+    half = pblk // 2
+    parts = half // 4
     ndiag, width = diag.shape
     piece = jax.ShapeDtypeStruct((rows, share), jnp.float32)
     whole = pltpu.VMEM((rows, share), jnp.float32)
@@ -277,11 +296,15 @@
     sems = pltpu.SemaphoreType.DMA
     return pl.pallas_call(
         functools.partial(gather_kernel, chunks),
-        out_shape=(piece, piece, jax.ShapeDtypeStruct((ndiag, width), jnp.float32)),
-        in_specs=[VMEM, VMEM, ANY, ANY],
-        out_specs=(ANY, ANY, VMEM),
+        out_shape=(
+            piece,
+            jax.ShapeDtypeStruct((pblk, BS, share), jnp.float32),
+            jax.ShapeDtypeStruct((ndiag, width), jnp.float32),
+        ),
+        in_specs=[SMEM, SMEM, SMEM, SMEM, VMEM, VMEM, ANY, ANY],
+        out_specs=(ANY, VMEM, VMEM),
         scratch_shapes=[
-            whole, whole, whole, whole, whole,
+            whole, whole, whole, whole, pltpu.VMEM((rows // BS, BS, share), jnp.float32),
             square, square, block, block,
             pltpu.VMEM((4, BS, BS), jnp.float32),
             pltpu.VMEM((BS, width), jnp.float32),
@@ -291,16 +314,22 @@
             pltpu.VMEM((4,) + mask.shape, jnp.float32),
             pltpu.VMEM((4,) + mask.shape, jnp.float32),
             pltpu.VMEM((2, tile, share), jnp.float32),
-            pltpu.VMEM((2, tile, share), jnp.float32),
+            pltpu.VMEM((4, pblk, BS, share), jnp.float32),
+            pltpu.VMEM((2, half, BS, share), jnp.float32),
+            pltpu.VMEM((2, half, BS, share), jnp.float32),
+            pltpu.VMEM((half, BS, share), jnp.float32),
+            pltpu.VMEM((half, BS, share), jnp.float32),
             sems((7,)), sems((7,)),
             sems((chunks,)), sems((chunks,)), sems((chunks,)), sems((chunks,)),
             sems, sems, sems((2,)), sems((2,)), sems((3,)), sems((3,)),
-            sems((4,)), sems((2,)), sems((2, 2)),
+            sems((4,)), sems((2,)), sems((2,)),
+            sems((2, parts)), sems((2, parts)), sems((2, parts)), sems((2, parts)),
+            sems((parts,)), sems((parts,)), sems((parts,)), sems((parts,)),
         ],
         compiler_params=pltpu.CompilerParams(
-            collective_id=0, has_side_effects=True, vmem_limit_bytes=48 * 2**20),
+            collective_id=0, has_side_effects=True, vmem_limit_bytes=58 * 2**20),
         name="gather_factor",
-    )(diag, mask, panel, contribution)
+    )(*chains, diag, mask, panel, contribution.reshape(rows // BS, BS, share))
 
 
 def split(value):
@@ -308,55 +337,13 @@
     return high, (value - high.astype(jnp.float32)).astype(jnp.bfloat16)
 
 
-def pack_kernel(tile, pblk, route_ref, slot_ref, f_in, u_ref, f_ref, t_ref):
-    step = pl.program_id(0)
-
-    @pl.when(step == 0)
-    def _():
-        t_ref[...] = jnp.zeros_like(t_ref)
-
-    f_ref[...] = f_in[...]
-    for b in range(tile // BS):
-        at = step * (tile // BS) + b
-        goal = route_ref[at] * pblk + slot_ref[at]
-        t_ref[goal] = t_ref[goal] + u_ref[b * BS:(b + 1) * BS, :]
-
-
-def pack_blocks(route, slot, factor, update, slots, pblk):
-    tile = 1024
-    rows, share = factor.shape
-    block = pl.BlockSpec((tile, share), lambda i, g, s: (i, 0))
-    return pl.pallas_call(
-        functools.partial(pack_kernel, tile, pblk),
-        out_shape=(
-            jax.ShapeDtypeStruct((rows, share), jnp.float32),
-            jax.ShapeDtypeStruct((slots, BS, share), jnp.float32),
-        ),
-        grid_spec=pltpu.PrefetchScalarGridSpec(
-            num_scalar_prefetch=2,
-            grid=(rows // tile,),
-            in_specs=[block] * 2,
-            out_specs=(block, pl.BlockSpec((slots, BS, share), lambda i, g, s: (0, 0, 0))),
-        ),
-        compiler_params=pltpu.CompilerParams(dimension_semantics=("arbitrary",)),
-        name="pack_blocks",
-    )(route, slot, factor, update)
-
-
-def route_kernel(t_ref, out_ref, ra, rb, ra2, rb2, asend, arecv, bsend, brecv,
-                 a2send, a2recv, b2send, b2recv):
-    z, r = lax.axis_index("cube"), lax.axis_index("row")
-    m, y = z % 2, 1 - r
-    dev_y = {"row": y}
-    dev_z = {"cube": z + 1 - 2 * m}
-    barrier = pltpu.get_barrier_semaphore()
-    for device in (dev_y, dev_z):
-        pl.semaphore_signal(barrier, inc=1, device_id=device, device_id_type=MESH)
-    pl.semaphore_wait(barrier, 2)
-    half = t_ref.shape[1] // 2
-    n = 8
+def route_slots(m, r, y, dev_y, dev_z, fill, t_ref, out_ref, ra, rb, ra2, rb2,
+                asend, arecv, bsend, brecv, a2send, a2recv, b2send, b2recv):
+    slots = t_ref.shape[1]
+    half = slots // 2
+    n = 4
     parts = half // n
-    over_a, over_b = {}, {}
+    over_a, over_b, last = {}, {}, {}
     for rel in range(2):
         for k in range(parts):
             h = (1 - m) if rel == 0 else m
@@ -367,9 +354,16 @@
             over_b[rel, k] = remote(
                 t_ref.at[(1 - m) * 2 + rr, pl.ds(half + k * n, n)], rb.at[rel, pl.ds(k * n, n)],
                 bsend.at[rel, k], brecv.at[rel, k], dev_z)
-            over_a[rel, k].start()
-            over_b[rel, k].start()
-    last = {}
+    fill(1 - m, y, 0, slots)
+    for k in range(parts):
+        over_a[0, k].start()
+        over_b[0, k].start()
+    fill(m, y, 0, slots)
+    fill(1 - m, r, 0, slots)
+    for k in range(parts):
+        over_a[1, k].start()
+        over_b[1, k].start()
+    fill(m, r, 0, slots)
     for k in range(parts):
         part = pl.ds(k * n, n)
         other = pl.ds(half + k * n, n)
@@ -399,43 +393,24 @@
         copy.wait_send()
 
 
-def route_blocks(packed):
-    _, slots, rows, share = packed.shape
-    half = slots // 2
-    parts = half // 8
-    return pl.pallas_call(
-        route_kernel,
-        out_shape=jax.ShapeDtypeStruct((slots, rows, share), jnp.float32),
-        in_specs=[VMEM],
-        out_specs=VMEM,
-        scratch_shapes=[
-            pltpu.VMEM((2, half, rows, share), jnp.float32),
-            pltpu.VMEM((2, half, rows, share), jnp.float32),
-            pltpu.VMEM((half, rows, share), jnp.float32),
-            pltpu.VMEM((half, rows, share), jnp.float32),
-            pltpu.SemaphoreType.DMA((2, parts)),
-            pltpu.SemaphoreType.DMA((2, parts)),
-            pltpu.SemaphoreType.DMA((2, parts)),
-            pltpu.SemaphoreType.DMA((2, parts)),
-            pltpu.SemaphoreType.DMA((parts,)),
-            pltpu.SemaphoreType.DMA((parts,)),
-            pltpu.SemaphoreType.DMA((parts,)),
-            pltpu.SemaphoreType.DMA((parts,)),
-        ],
-        compiler_params=pltpu.CompilerParams(collective_id=1, has_side_effects=True),
-        name="route_blocks",
-    )(packed)
-
-
 def on_small(diag_block, panel, pattern, contribution, route, slot):
     rows, share = panel.shape[1:]
     blk = rows // BS
     pblk = blk // 2
     nrow = lax.axis_size("row")
     mask = jnp.broadcast_to(pattern[0].astype(jnp.float32), (blk, share))
-    factor, update, lower = gather_and_factor(diag_block[0], mask, panel[0], contribution[0])
-    factor, packed = pack_blocks(route[0, :, 0], slot[0], factor, update, 2 * nrow * pblk, pblk)
-    assembled = route_blocks(packed.reshape(2 * nrow, pblk, BS, share))
+    goal = (route[0, :, 0] * pblk + slot[0]).astype(jnp.int32)
+    ids = jnp.arange(blk, dtype=jnp.int32)
+    earlier = (goal[None, :] == goal[:, None]) & (ids[None, :] < ids[:, None])
+    prev = jnp.max(jnp.where(earlier, ids[None, :] + 1, 0), axis=1)
+    names = jnp.arange(2 * nrow * pblk, dtype=jnp.int32)
+    last = jnp.max(jnp.where(goal[None, :] == names[:, None], ids[None, :] + 1, 0), axis=1)
+    chains = (
+        jnp.maximum(prev - 1, 0), jnp.minimum(prev, 1).astype(jnp.float32),
+        jnp.maximum(last - 1, 0), jnp.minimum(last, 1).astype(jnp.float32),
+    )
+    factor, assembled, lower = factor_and_route(
+        chains, diag_block[0], mask, panel[0], contribution[0], pblk)
     return (lower[None], factor[None], assembled.reshape(1, pblk * BS, share))
 
 

time: 197 us -> 186 us (0.944)
  Pallas kernels: 189 us -> 174 us
  other arithmetic: 0.66 us -> 3.34 us
    pallas_call x3 -> x1, Pallas kernels: 189 us -> 174 us  [factor_and_route(): pl.pallas_call(functools.partial(gather_kernel, chunks), out_shape=(piece...]
    unnamed x6 -> x5, local copies, waits for them, and re-layouts: 6.54 us -> 7.51 us
where the time goes in v3:
time: 186 us
  Pallas kernels  174 us (94%)
  local copies, waits for them, and re-layouts  8.2 us (4%)
  other arithmetic  3.34 us (2%)
    pallas_call x1, Pallas kernels, factor_and_route(): pl.pallas_call(functools.partial(gather_kernel, chunks), out_shape=(piece...  174 us
    unnamed x5, local copies, waits for them, and re-layouts  7.51 us

profile of v3, /device:TPU:0, one launch (start us, length us, event | category | flops | bytes accessed | tf_op | source)
XLA Modules:
  0.0 186.1 jit_solution(10369550597107251963)
XLA Ops:
  0.6 0.7 fusion.1
  1.3 0.7 convert_bitcast_fusion
  2.0 0.7 bitcast_add_fusion
  2.6 0.2 select_reduce_fusion.1
  2.8 0.1 select_reduce_fusion
  2.9 0.5 minimum_convert_fusion
  3.5 0.5 minimum_convert_fusion.1
  4.0 0.7 broadcast_in_dim.47.mask_ref
  4.7 173.9 %gather_factor.1 = (f32[8192,128]{1,0:T(8,128)}, f32[32,128,128]{2,1,0:T(8,128)}, f32[64,512]{1,0:T(8,128)}) custom-call(s32[64]{0:T(128)} %get-tuple-element.12.prev_ref, f32[64]{0:T(128)} %get-tuple-element.11.prev_on, s32[128]{0:T(128)} %get-tuple-element.10.last_ref, f32[128]{0:T(128)} %get-tuple-element.9.last_on, f32[64,512]{1,0:T(8,128)} %bitcast.22, ...), custom_call_target="tpu_custom_call" | custom-call | tf_op jit(solution)/shard_map/gather_factor/pallas_call | solution.py:297
  178.6 1.6 copy.12
  180.1 0.0 copy-start
  180.1 4.6 %copy.13 = f32[1,8192,128]{2,1,0:T(8,128)} copy(f32[1,8192,128]{2,1,0:T(8,128)} %bitcast.20) | data formatting | bytes 8388608
  184.8 0.0 copy-done
  184.8 1.3 copy.14
Async XLA Ops:
  180.1 4.6 %copy-start = (f32[32,128,128]{2,1,0:T(8,128)S(1)}, f32[32,128,128]{2,1,0:T(8,128)}, u32[]{:S(2)}) copy-start(f32[32,128,128]{2,1,0:T(8,128)} %get-tuple-element.8) | copy-start | bytes 6291460
